TPU v7x, 1024 devices: a whole 4x8x16 slice. The times are simulated.
1024 devices in a mesh: seq: 32 (over x, y_hi, core), chan: 32 (over z, y_lo).
Axes of the slice: x: 4, y: 8 (y_hi: 4, y_lo: 2; y = y_hi * 2 + y_lo), z: 16, core: 2. Of those that a mesh axis runs over, the one named last changes fastest.
Arguments:
- query_proj: bfloat16 [4096, 4096], P('chan', 'seq'), may hold values from -6 to 6
- key_proj: bfloat16 [4096, 4096], P('chan', 'seq'), may hold values from -6 to 6
- value_proj: bfloat16 [4096, 4096], P('chan', 'seq'), may hold values from -6 to 6
- cotangent: bfloat16 [4096, 4096], P('chan', 'seq'), may hold values from -6 to 6
- filter_taps: bfloat16 [128, 4096], P('seq'), may hold values from -6 to 6
Outputs:
- gated_out: bfloat16 [4096, 4096], P('chan', 'seq')
- query_grad: bfloat16 [4096, 4096], P('chan', 'seq')
- key_grad: bfloat16 [4096, 4096], P('chan', 'seq')
- value_grad: bfloat16 [4096, 4096], P('chan', 'seq')
- filter_grad: float32 [128, 4096], P('seq', 'chan')
All inputs are finite; a program needn't handle non-finite values.
Results may differ from a plain program's by a relative error of at most 0.0057.
Values may be sent and summed in bfloat16 or wider, within the bound.
A program may use at most 32 MiB of HBM per device.

v0:
```python
import functools
import math

import jax
import jax.numpy as jnp
from jax import lax
from jax.experimental import pallas as pl
from jax.experimental.pallas import tpu as pltpu
from jax.sharding import PartitionSpec as P

MESH = pl.DeviceIdType.MESH
F32 = jnp.float32
BF16 = jnp.bfloat16
W = 128
CH = 4


def flip_matrix():
    row = lax.broadcasted_iota(jnp.int32, (W, W), 0)
    col = lax.broadcasted_iota(jnp.int32, (W, W), 1)
    return jnp.where(row + col == W - 1, 1.0, 0.0).astype(BF16)


def dot(left, right):
    return jnp.dot(left, right, preferred_element_type=F32)


def write_toeplitz(blocks, row_of, out_ref):
    row = lax.broadcasted_iota(jnp.int32, (W, W), 0)
    col = lax.broadcasted_iota(jnp.int32, (W, W), 1)
    lower = row >= col
    before = jnp.zeros((W, W), F32)
    for k in range(blocks):
        turned = pltpu.roll(
            jnp.broadcast_to(row_of(k), (W, W)), 1, 1, stride=1, stride_axis=0
        )
        out_ref[W * k : W * (k + 1), :] = jnp.where(lower, turned, before).astype(BF16)
        before = turned


def kernel(
    n, scale,
    q_hbm, k_hbm, v_hbm, g_hbm, taps_hbm,
    gated_ref, qgrad_ref, kgrad_ref, vgrad_ref, fgrad_ref,
    q, k, v, g, taps, in_sem,
    send1, recv1, send2, recv2, send3, recv3, sems,
    tap_rows, tap_flip, wide1, flip1, pad_p, pad_x, filt_toe, x_toe, lhs, wide2,
):
    me_seq = lax.axis_index("seq")
    me_chan = lax.axis_index("chan")

    loads = [
        pltpu.make_async_copy(src, dst, in_sem.at[i])
        for i, (src, dst) in enumerate(
            ((k_hbm, k), (v_hbm, v), (g_hbm, g), (q_hbm, q), (taps_hbm, taps))
        )
    ]
    for load in loads:
        load.start()

    barrier = pltpu.get_barrier_semaphore()

    def greet(i, carry):
        pl.semaphore_signal(
            barrier, inc=1, device_id={"seq": lax.rem(me_seq + i, n)}, device_id_type=MESH
        )
        pl.semaphore_signal(
            barrier, inc=1, device_id={"chan": lax.rem(me_chan + i, n)}, device_id_type=MESH
        )
        return carry

    lax.fori_loop(1, n, greet, 0)

    half = lax.broadcasted_iota(jnp.int32, (CH * n // 8, 8, W), 1) < CH

    def swap(x):
        return pltpu.roll(x, CH, 1)

    for load in loads[:4]:
        load.wait()
    tiles = (CH * n // 8, 8, W)
    mixed = (k[...].astype(F32) * v[...].astype(F32)).reshape(tiles)
    pulled = (g[...].astype(F32) * q[...].astype(F32)).reshape(tiles)
    pair = jnp.stack(
        [jnp.where(half, mixed, swap(pulled)), jnp.where(half, swap(mixed), pulled)], axis=1
    )
    send1[...] = pair.reshape(n, 8, W).astype(BF16)

    pl.semaphore_wait(barrier, 2 * (n - 1))

    def exchange(axis, me, send, recv, at):
        def step(i, carry):
            to = lax.rem(me + i, n)
            pltpu.make_async_remote_copy(
                src_ref=send.at[to], dst_ref=recv.at[me],
                send_sem=sems.at[at], recv_sem=sems.at[at + 1],
                device_id={axis: to}, device_id_type=MESH,
            ).start()
            return carry

        lax.fori_loop(1, n, step, 0)
        recv[me] = send[me]

    def all_of(axis, me, send, recv, at):
        return pltpu.make_async_remote_copy(
            src_ref=send.at[pl.ds(0, n - 1)], dst_ref=recv.at[pl.ds(0, n - 1)],
            send_sem=sems.at[at], recv_sem=sems.at[at + 1],
            device_id={axis: lax.rem(me + 1, n)}, device_id_type=MESH,
        )

    exchange("seq", me_seq, send1, recv1, 0)

    flip = flip_matrix()
    loads[4].wait()
    tap_values = taps[...].astype(F32)
    for b in range(n):
        tap_rows[CH * b : CH * (b + 1), :] = tap_values[:, W * b : W * (b + 1)]
    tap_flip[...] = dot(tap_rows[...].astype(BF16), flip)

    def filter_matrix(c, carry):
        write_toeplitz(n, lambda b: tap_flip[pl.ds(CH * b + c, 1), :], filt_toe.at[c])
        return carry

    lax.fori_loop(0, CH, filter_matrix, 0)
    pad_p[...] = jnp.zeros_like(pad_p)
    pad_x[...] = jnp.zeros_like(pad_x)

    all_of("seq", me_seq, send1, recv1, 0).wait_recv()
    got = recv1[...].reshape(n * 8, W)
    wide1[...] = got.astype(F32)
    flip1[...] = dot(got, flip)

    def convolve(c, carry):
        pad_p[:n, :] = wide1[pl.ds(CH + c, n, stride=8), :]
        pad_x[n:, :] = flip1[pl.ds(c, n, stride=8), :]
        for b in range(n):
            lhs[c, :n, W * b : W * (b + 1)] = pad_p[b : b + n, :].astype(BF16)
            lhs[c, n:, W * b : W * (b + 1)] = pad_x[n - b : 2 * n - b, :].astype(BF16)
        both = dot(lhs[c], filt_toe[c]) * scale
        wide2[pl.ds(c, n, stride=8), :] = both[n:]
        wide2[pl.ds(CH + c, n, stride=8), :] = both[:n]
        return carry

    lax.fori_loop(0, CH, convolve, 0)
    send2[...] = wide2[...].reshape(n, 8, W).astype(BF16)
    exchange("seq", me_seq, send2, recv2, 2)

    def lags(c, carry):
        write_toeplitz(n, lambda b: flip1[pl.ds(8 * b + c, 1), :], x_toe)
        wide2[pl.ds(c, n, stride=8), :] = dot(lhs[c, :n, :], x_toe[...]) * scale
        return carry

    lax.fori_loop(0, CH, lags, 0)
    send3[...] = wide2[...].reshape(n, 8, W)[:, :CH, :]
    exchange("chan", me_chan, send3, recv3, 4)

    all_of("seq", me_seq, send2, recv2, 2).wait_recv()
    came = recv2[...].astype(F32).reshape(CH * n // 8, 2, 8, W)
    low, high = came[:, 0], came[:, 1]
    conv = jnp.where(half, low, swap(high)).reshape(CH * n, W)
    back = jnp.where(half, swap(low), high).reshape(CH * n, W)
    conv = dot(conv.astype(BF16), flip)
    gated_ref[...] = (q[...].astype(F32) * conv).astype(BF16)
    qgrad_ref[...] = (g[...].astype(F32) * conv).astype(BF16)
    kgrad_ref[...] = (back * v[...].astype(F32)).astype(BF16)
    vgrad_ref[...] = (back * k[...].astype(F32)).astype(BF16)

    all_of("chan", me_chan, send3, recv3, 4).wait_recv()
    fgrad_ref[...] = jnp.sum(recv3[...], axis=0)

    all_of("seq", me_seq, send1, recv1, 0).wait_send()
    all_of("seq", me_seq, send2, recv2, 2).wait_send()
    all_of("chan", me_chan, send3, recv3, 4).wait_send()


def on_device(n, query_proj, key_proj, value_proj, cotangent, filter_taps):
    rows = CH * n
    length = W * n
    vmem = pl.BlockSpec(memory_space=pltpu.VMEM)
    hbm = pl.BlockSpec(memory_space=pltpu.HBM)
    slab = jax.ShapeDtypeStruct((rows, W), BF16)
    return pl.pallas_call(
        functools.partial(kernel, n, 1.0 / math.sqrt(length)),
        out_shape=(slab, slab, slab, slab, jax.ShapeDtypeStruct((CH, W), F32)),
        in_specs=[hbm] * 5,
        out_specs=(vmem,) * 5,
        scratch_shapes=[pltpu.VMEM((rows, W), BF16)] * 4
        + [
            pltpu.VMEM((CH, length), BF16),
            pltpu.SemaphoreType.DMA((5,)),
            pltpu.VMEM((n, 8, W), BF16),
            pltpu.VMEM((n, 8, W), BF16),
            pltpu.VMEM((n, 8, W), BF16),
            pltpu.VMEM((n, 8, W), BF16),
            pltpu.VMEM((n, CH, W), F32),
            pltpu.VMEM((n, CH, W), F32),
            pltpu.SemaphoreType.DMA((6,)),
            pltpu.VMEM((rows, W), F32),
            pltpu.VMEM((rows, W), F32),
            pltpu.VMEM((8 * n, W), F32),
            pltpu.VMEM((8 * n, W), F32),
            pltpu.VMEM((2 * n, W), F32),
            pltpu.VMEM((2 * n, W), F32),
            pltpu.VMEM((CH, length, W), BF16),
            pltpu.VMEM((length, W), BF16),
            pltpu.VMEM((CH, 2 * n, length), BF16),
            pltpu.VMEM((8 * n, W), F32),
        ],
        compiler_params=pltpu.CompilerParams(
            collective_id=0, has_side_effects=True, vmem_limit_bytes=32 << 20
        ),
    )(*(pltpu.with_memory_space_constraint(x, pltpu.HBM) for x in (query_proj, key_proj, value_proj, cotangent, filter_taps)))


def solution(mesh):
    return jax.shard_map(
        functools.partial(on_device, mesh.shape["seq"]),
        mesh=mesh,
        in_specs=(
            P("chan", "seq"),
            P("chan", "seq"),
            P("chan", "seq"),
            P("chan", "seq"),
            P("seq", None),
        ),
        out_specs=(
            P("chan", "seq"),
            P("chan", "seq"),
            P("chan", "seq"),
            P("chan", "seq"),
            P("seq", "chan"),
        ),
        check_vma=False,
    )
```

profile of v0, /device:TPU:1, one launch (start us, length us, event | category | flops | bytes accessed | tf_op | source)
XLA Modules:
  0.0 47.1 jit_solution(8381870321093381586)
XLA Ops:
  0.6 43.4 %shard_map.92 = (bf16[128,128]{1,0:T(8,128)(2,1)S(1)}, bf16[128,128]{1,0:T(8,128)(2,1)S(1)}, bf16[128,128]{1,0:T(8,128)(2,1)S(1)}, bf16[128,128]{1,0:T(8,128)(2,1)S(1)}, f32[4,128]{1,0:T(4,128)S(1)}) custom-call(bf16[128,128]{1,0:T(8,128)(2,1)} %q_hbm.1, bf16[128,128]{1,0:T(8,128)(2,1)} %k_hbm.1, bf16[128,128]{1,0:T(8,128)(2,1)} %v_hbm.1, ...), custom_call_target="tpu_custom_call" | custom-call | tf_op jit(solution)/shard_map/pallas_call | solution.py:182
  44.1 0.6 %copy.15 = bf16[128,128]{1,0:T(8,128)(2,1)} copy(bf16[128,128]{1,0:T(8,128)(2,1)S(1)} %get-tuple-element.10) | data formatting | bytes 65536
  44.7 0.6 %copy.16 = bf16[128,128]{1,0:T(8,128)(2,1)} copy(bf16[128,128]{1,0:T(8,128)(2,1)S(1)} %get-tuple-element.11) | data formatting | bytes 65536
  45.3 0.6 %copy.17 = bf16[128,128]{1,0:T(8,128)(2,1)} copy(bf16[128,128]{1,0:T(8,128)(2,1)S(1)} %get-tuple-element.12) | data formatting | bytes 65536
  45.9 0.6 %copy.18 = bf16[128,128]{1,0:T(8,128)(2,1)} copy(bf16[128,128]{1,0:T(8,128)(2,1)S(1)} %get-tuple-element.13) | data formatting | bytes 65536
  46.5 0.6 %copy.19 = f32[4,128]{1,0:T(4,128)} copy(f32[4,128]{1,0:T(4,128)S(1)} %get-tuple-element.14) | data formatting | bytes 4096
where the time goes:
time: 47.3 us; the launch traced here: 47.1 us
  Pallas kernels  43.4 us (92%)
  local copies, waits for them, and re-layouts  3.04 us (6%)
  between operations  0.64 us (1%)
    pallas_call x1, Pallas kernels, on_device(): pl.pallas_call(functools.partial(kernel, n, 1.0 / math.sqrt(length)), out...  43.4 us
    unnamed x5, local copies, waits for them, and re-layouts  3.04 us

commit v1 on v0

v1 whole, which is shorter than its diff:
```python
import functools
import math

import jax
import jax.numpy as jnp
from jax import lax
from jax.experimental import pallas as pl
from jax.experimental.pallas import tpu as pltpu
from jax.sharding import PartitionSpec as P

MESH = pl.DeviceIdType.MESH
F32 = jnp.float32
BF16 = jnp.bfloat16
W = 128
CH = 4


def flip_matrix():
    row = lax.broadcasted_iota(jnp.int32, (W, W), 0)
    col = lax.broadcasted_iota(jnp.int32, (W, W), 1)
    return jnp.where(row + col == W - 1, 1.0, 0.0).astype(BF16)


def dot(left, right):
    return jnp.dot(left, right, preferred_element_type=F32)


def toeplitz_sum(blocks, row_of, left_of):
    row = lax.broadcasted_iota(jnp.int32, (W, W), 0)
    col = lax.broadcasted_iota(jnp.int32, (W, W), 1)
    lower = row >= col
    before = jnp.zeros((W, W), F32)
    total = None
    for k in range(0, blocks, 2):
        parts = []
        for b in (k, k + 1):
            turned = pltpu.roll(
                jnp.broadcast_to(row_of(b), (W, W)), 1, 1, stride=1, stride_axis=0
            )
            parts.append(jnp.where(lower, turned, before).astype(BF16))
            before = turned
        left = jnp.concatenate([left_of(k), left_of(k + 1)], axis=1)
        term = dot(left, jnp.concatenate(parts, axis=0))
        total = term if total is None else total + term
    return total


def kernel(
    n, scale,
    q_hbm, k_hbm, v_hbm, g_hbm, taps_hbm,
    gated_ref, qgrad_ref, kgrad_ref, vgrad_ref, fgrad_ref,
    q, k, v, g, taps, in_sem,
    send1, recv1, send2, recv2, send3, recv3, sems, all_seq, all_chan,
    tap_rows, tap_flip, wide1, pad_p, pad_x, wide2, wide3,
):
    me_seq = lax.axis_index("seq")
    me_chan = lax.axis_index("chan")
    core = lax.rem(me_seq, 2)
    pair = me_seq + 1 - 2 * core
    late = me_chan >= n // 2

    loads = [
        pltpu.make_async_copy(src, dst, in_sem.at[i])
        for i, (src, dst) in enumerate(
            ((k_hbm, k), (v_hbm, v), (g_hbm, g), (q_hbm, q), (taps_hbm, taps))
        )
    ]
    for load in loads:
        load.start()

    barrier = pltpu.get_barrier_semaphore()

    def tell(sem, **to):
        pl.semaphore_signal(sem, inc=1, device_id=to, device_id_type=MESH)

    def greet_seq(i, carry):
        tell(barrier, seq=lax.rem(me_seq - core + 2 * i, n))
        return carry

    lax.fori_loop(1, n // 2, greet_seq, 0)

    @pl.when(core == 1)
    def _():
        tell(barrier, seq=pair)

    half = lax.broadcasted_iota(jnp.int32, (CH * n // 8, 8, W), 1) < CH
    flip = flip_matrix()

    def swap(x):
        return pltpu.roll(x, CH, 1)

    for load in loads[:4]:
        load.wait()
    tiles = (CH * n // 8, 8, W)
    mixed = (k[...].astype(F32) * v[...].astype(F32)).astype(BF16)
    mixed = dot(mixed, flip).reshape(tiles)
    pulled = (g[...].astype(F32) * q[...].astype(F32)).reshape(tiles)
    paired = jnp.stack(
        [jnp.where(half, mixed, swap(pulled)), jnp.where(half, swap(mixed), pulled)], axis=1
    )
    send1[...] = paired.reshape(n, 8, W).astype(BF16)

    @pl.when(core == 0)
    def _():
        pl.semaphore_wait(barrier, n - 1)
        tell(all_seq, seq=pair)

    @pl.when(core == 1)
    def _():
        pl.semaphore_wait(all_seq, 1)

    def exchange(axis, me, send, recv, at):
        def step(i, carry):
            to = lax.rem(me + i, n)
            pltpu.make_async_remote_copy(
                src_ref=send.at[to], dst_ref=recv.at[me],
                send_sem=sems.at[at], recv_sem=sems.at[at + 1],
                device_id={axis: to}, device_id_type=MESH,
            ).start()
            return carry

        lax.fori_loop(1, n, step, 0)
        recv[me] = send[me]

    def all_of(axis, me, send, recv, at):
        return pltpu.make_async_remote_copy(
            src_ref=send.at[pl.ds(0, n - 1)], dst_ref=recv.at[pl.ds(0, n - 1)],
            send_sem=sems.at[at], recv_sem=sems.at[at + 1],
            device_id={axis: lax.rem(me + 1, n)}, device_id_type=MESH,
        )

    exchange("seq", me_seq, send1, recv1, 0)

    @pl.when(core == 1)
    def _():
        def greet_chan(i, carry):
            tell(barrier, chan=lax.rem(me_chan + i, n))
            return carry

        lax.fori_loop(1, n, greet_chan, 0)

    pad_p[...] = jnp.zeros_like(pad_p)
    pad_x[...] = jnp.zeros_like(pad_x)

    all_of("seq", me_seq, send1, recv1, 0).wait_recv()
    wide1[...] = recv1[...].reshape(n * 8, W).astype(F32)
    for c in range(CH):
        pad_p[c, :n, :] = wide1[pl.ds(CH + c, n, stride=8), :]
        pad_x[c, n:, :] = wide1[pl.ds(c, n, stride=8), :]

    def lags(c, carry):
        wide3[pl.ds(c, n, stride=8), :] = scale * toeplitz_sum(
            n,
            lambda b: pad_x[c, pl.ds(n + b, 1), :],
            lambda b: pad_p[c, b : b + n, :].astype(BF16),
        )
        return carry

    lax.fori_loop(0, CH, lags, 0)
    send3[...] = wide3[...].reshape(n, 8, W)[:, :CH, :]

    def exchange_lags():
        @pl.when(core == 1)
        def _():
            pl.semaphore_wait(barrier, n - 1)
            tell(all_chan, seq=pair)

        @pl.when(core == 0)
        def _():
            pl.semaphore_wait(all_chan, 1)

        exchange("chan", me_chan, send3, recv3, 4)

    pl.when(late)(exchange_lags)

    loads[4].wait()
    tap_values = taps[...].astype(F32)
    for b in range(n):
        tap_rows[CH * b : CH * (b + 1), :] = tap_values[:, W * b : W * (b + 1)]
    tap_flip[...] = dot(tap_rows[...].astype(BF16), flip)

    def convolve(c, carry):
        both = scale * toeplitz_sum(
            n,
            lambda b: tap_flip[pl.ds(CH * b + c, 1), :],
            lambda b: jnp.concatenate(
                [
                    pad_p[c, b : b + n, :].astype(BF16),
                    pad_x[c, n - b : 2 * n - b, :].astype(BF16),
                ],
                axis=0,
            ),
        )
        wide2[pl.ds(c, n, stride=8), :] = both[n:]
        wide2[pl.ds(CH + c, n, stride=8), :] = both[:n]
        return carry

    lax.fori_loop(0, CH, convolve, 0)
    send2[...] = wide2[...].reshape(n, 8, W).astype(BF16)
    exchange("seq", me_seq, send2, recv2, 2)

    all_of("seq", me_seq, send2, recv2, 2).wait_recv()
    came = recv2[...].astype(F32).reshape(CH * n // 8, 2, 8, W)
    low, high = came[:, 0], came[:, 1]
    conv = jnp.where(half, low, swap(high)).reshape(CH * n, W)
    back = jnp.where(half, swap(low), high).reshape(CH * n, W)
    conv = dot(conv.astype(BF16), flip)
    gated_ref[...] = (q[...].astype(F32) * conv).astype(BF16)
    qgrad_ref[...] = (g[...].astype(F32) * conv).astype(BF16)
    kgrad_ref[...] = (back * v[...].astype(F32)).astype(BF16)
    vgrad_ref[...] = (back * k[...].astype(F32)).astype(BF16)

    pl.when(jnp.logical_not(late))(exchange_lags)

    all_of("seq", me_seq, send1, recv1, 0).wait_send()
    all_of("seq", me_seq, send2, recv2, 2).wait_send()
    all_of("chan", me_chan, send3, recv3, 4).wait_send()
    all_of("chan", me_chan, send3, recv3, 4).wait_recv()
    fgrad_ref[...] = jnp.sum(recv3[...], axis=0)


def write_out(*refs):
    count = (len(refs) - 1) // 2
    sem = refs[-1]
    copies = [
        pltpu.make_async_copy(refs[i], refs[count + i], sem.at[i]) for i in range(count)
    ]
    for copy in copies:
        copy.start()
    for copy in copies:
        copy.wait()


def on_device(n, *args):
    rows = CH * n
    length = W * n
    vmem = pl.BlockSpec(memory_space=pltpu.VMEM)
    hbm = pl.BlockSpec(memory_space=pltpu.HBM)
    slab = jax.ShapeDtypeStruct((rows, W), BF16)
    shapes = (slab, slab, slab, slab, jax.ShapeDtypeStruct((CH, W), F32))
    results = pl.pallas_call(
        functools.partial(kernel, n, 1.0 / math.sqrt(length)),
        out_shape=shapes,
        in_specs=[hbm] * 5,
        out_specs=(vmem,) * 5,
        scratch_shapes=[pltpu.VMEM((rows, W), BF16)] * 4
        + [
            pltpu.VMEM((CH, length), BF16),
            pltpu.SemaphoreType.DMA((5,)),
            pltpu.VMEM((n, 8, W), BF16),
            pltpu.VMEM((n, 8, W), BF16),
            pltpu.VMEM((n, 8, W), BF16),
            pltpu.VMEM((n, 8, W), BF16),
            pltpu.VMEM((n, CH, W), F32),
            pltpu.VMEM((n, CH, W), F32),
            pltpu.SemaphoreType.DMA((6,)),
            pltpu.SemaphoreType.REGULAR,
            pltpu.SemaphoreType.REGULAR,
            pltpu.VMEM((rows, W), F32),
            pltpu.VMEM((rows, W), F32),
            pltpu.VMEM((8 * n, W), F32),
            pltpu.VMEM((CH, 2 * n, W), F32),
            pltpu.VMEM((CH, 2 * n, W), F32),
            pltpu.VMEM((8 * n, W), F32),
            pltpu.VMEM((8 * n, W), F32),
        ],
        compiler_params=pltpu.CompilerParams(
            collective_id=0, has_side_effects=True, vmem_limit_bytes=32 << 20
        ),
    )(*(pltpu.with_memory_space_constraint(x, pltpu.HBM) for x in args))
    return pl.pallas_call(
        write_out,
        out_shape=shapes,
        in_specs=[vmem] * 5,
        out_specs=(hbm,) * 5,
        scratch_shapes=[pltpu.SemaphoreType.DMA((5,))],
    )(*(pltpu.with_memory_space_constraint(x, pltpu.VMEM) for x in results))


def solution(mesh):
    return jax.shard_map(
        functools.partial(on_device, mesh.shape["seq"]),
        mesh=mesh,
        in_specs=(
            P("chan", "seq"),
            P("chan", "seq"),
            P("chan", "seq"),
            P("chan", "seq"),
            P("seq", None),
        ),
        out_specs=(
            P("chan", "seq"),
            P("chan", "seq"),
            P("chan", "seq"),
            P("chan", "seq"),
            P("seq", "chan"),
        ),
        check_vma=False,
    )
```

time: 47.3 us -> 44.5 us (0.941)
  local copies, waits for them, and re-layouts: 3.04 us -> 0 us
    unnamed x5 -> x0, local copies, waits for them, and re-layouts: 3.04 us -> none
    pallas_call x0 -> x1, Pallas kernels: none -> 0.7 us  [on_device(): pl.pallas_call(write_out, out_shape=shapes, in_specs=[vmem] * 5, out_spec...]
where the time goes in v1:
time: 44.5 us; the launch traced here: 44.3 us
  Pallas kernels  43.7 us (98%)
  between operations  0.64 us (1%)
    pallas_call x1, Pallas kernels, on_device(): pl.pallas_call(functools.partial(kernel, n, 1.0 / math.sqrt(length)), out...  43 us

profile of v1, /device:TPU:1, one launch (start us, length us, event | category | flops | bytes accessed | tf_op | source)
XLA Modules:
  0.0 44.3 jit_solution(18019328404624812364)
XLA Ops:
  0.6 43.0 %shard_map.92 = (bf16[128,128]{1,0:T(8,128)(2,1)S(1)}, bf16[128,128]{1,0:T(8,128)(2,1)S(1)}, bf16[128,128]{1,0:T(8,128)(2,1)S(1)}, bf16[128,128]{1,0:T(8,128)(2,1)S(1)}, f32[4,128]{1,0:T(4,128)S(1)}) custom-call(bf16[128,128]{1,0:T(8,128)(2,1)} %q_hbm.1, bf16[128,128]{1,0:T(8,128)(2,1)} %k_hbm.1, bf16[128,128]{1,0:T(8,128)(2,1)} %v_hbm.1, ...), custom_call_target="tpu_custom_call" | custom-call | tf_op jit(solution)/shard_map/pallas_call | solution.py:241
  43.6 0.7 %shard_map.93 = (bf16[128,128]{1,0:T(8,128)(2,1)}, bf16[128,128]{1,0:T(8,128)(2,1)}, bf16[128,128]{1,0:T(8,128)(2,1)}, bf16[128,128]{1,0:T(8,128)(2,1)}, f32[4,128]{1,0:T(4,128)}) custom-call(bf16[128,128]{1,0:T(8,128)(2,1)S(1)} %get-tuple-element.10.refs_0_, bf16[128,128]{1,0:T(8,128)(2,1)S(1)} %get-tuple-element.11.refs_1_, ...), custom_call_target="tpu_custom_call" | custom-call | tf_op jit(solution)/shard_map/pallas_call | solution.py:271

commit v2 on v1

--- a/solution.py
+++ b/solution.py
@@ -73,15 +73,37 @@
     def tell(sem, **to):
         pl.semaphore_signal(sem, inc=1, device_id=to, device_id_type=MESH)
 
-    def greet_seq(i, carry):
-        tell(barrier, seq=lax.rem(me_seq - core + 2 * i, n))
-        return carry
-
-    lax.fori_loop(1, n // 2, greet_seq, 0)
+    chips = n // 2
+    outer = min(chips, 4)
+    inner = chips // outer
+    own = (inner // 2) * outer + outer // 2
+    my_outer, my_inner = me_seq // (2 * inner), lax.rem(me_seq // 2, inner)
+
+    def chip_at(i):
+        at_outer = lax.rem(my_outer + outer // 2 + lax.rem(i, outer), outer)
+        at_inner = lax.rem(my_inner + inner // 2 + i // outer, inner)
+        return 2 * (at_outer * inner + at_inner)
+
+    def each_other_chip(step):
+        def body(i, carry):
+            step(chip_at(i))
+            return carry
+
+        lax.fori_loop(0, own, body, 0)
+        lax.fori_loop(own + 1, chips, body, 0)
+
+    each_other_chip(lambda to: tell(barrier, seq=to))
 
     @pl.when(core == 1)
     def _():
         tell(barrier, seq=pair)
+
+    def greet_chan(i, carry):
+        tell(barrier, seq=me_seq - core + 1, chan=i)
+        return carry
+
+    lax.fori_loop(0, me_chan, greet_chan, 0)
+    lax.fori_loop(me_chan + 1, n, greet_chan, 0)
 
     half = lax.broadcasted_iota(jnp.int32, (CH * n // 8, 8, W), 1) < CH
     flip = flip_matrix()
@@ -109,18 +131,30 @@
     def _():
         pl.semaphore_wait(all_seq, 1)
 
-    def exchange(axis, me, send, recv, at):
+    def send_one(axis, me, to, send, recv, at):
+        pltpu.make_async_remote_copy(
+            src_ref=send.at[to], dst_ref=recv.at[me],
+            send_sem=sems.at[at], recv_sem=sems.at[at + 1],
+            device_id={axis: to}, device_id_type=MESH,
+        ).start()
+
+    def exchange_seq(send, recv, at):
+        def both_cores(to):
+            send_one("seq", me_seq, to, send, recv, at)
+            send_one("seq", me_seq, to + 1, send, recv, at)
+
+        each_other_chip(both_cores)
+        send_one("seq", me_seq, pair, send, recv, at)
+        recv[me_seq] = send[me_seq]
+
+    def exchange_chan(send, recv, at):
         def step(i, carry):
-            to = lax.rem(me + i, n)
-            pltpu.make_async_remote_copy(
-                src_ref=send.at[to], dst_ref=recv.at[me],
-                send_sem=sems.at[at], recv_sem=sems.at[at + 1],
-                device_id={axis: to}, device_id_type=MESH,
-            ).start()
+            send_one("chan", me_chan, i, send, recv, at)
             return carry
 
-        lax.fori_loop(1, n, step, 0)
-        recv[me] = send[me]
+        lax.fori_loop(0, me_chan, step, 0)
+        lax.fori_loop(me_chan + 1, n, step, 0)
+        recv[me_chan] = send[me_chan]
 
     def all_of(axis, me, send, recv, at):
         return pltpu.make_async_remote_copy(
@@ -129,15 +163,7 @@
             device_id={axis: lax.rem(me + 1, n)}, device_id_type=MESH,
         )
 
-    exchange("seq", me_seq, send1, recv1, 0)
-
-    @pl.when(core == 1)
-    def _():
-        def greet_chan(i, carry):
-            tell(barrier, chan=lax.rem(me_chan + i, n))
-            return carry
-
-        lax.fori_loop(1, n, greet_chan, 0)
+    exchange_seq(send1, recv1, 0)
 
     pad_p[...] = jnp.zeros_like(pad_p)
     pad_x[...] = jnp.zeros_like(pad_x)
@@ -148,28 +174,25 @@
         pad_p[c, :n, :] = wide1[pl.ds(CH + c, n, stride=8), :]
         pad_x[c, n:, :] = wide1[pl.ds(c, n, stride=8), :]
 
-    def lags(c, carry):
+    for c in range(CH):
         wide3[pl.ds(c, n, stride=8), :] = scale * toeplitz_sum(
             n,
             lambda b: pad_x[c, pl.ds(n + b, 1), :],
             lambda b: pad_p[c, b : b + n, :].astype(BF16),
         )
-        return carry
-
-    lax.fori_loop(0, CH, lags, 0)
     send3[...] = wide3[...].reshape(n, 8, W)[:, :CH, :]
 
     def exchange_lags():
         @pl.when(core == 1)
         def _():
-            pl.semaphore_wait(barrier, n - 1)
+            pl.semaphore_wait(barrier, 2 * (n - 1))
             tell(all_chan, seq=pair)
 
         @pl.when(core == 0)
         def _():
             pl.semaphore_wait(all_chan, 1)
 
-        exchange("chan", me_chan, send3, recv3, 4)
+        exchange_chan(send3, recv3, 4)
 
     pl.when(late)(exchange_lags)
 
@@ -179,7 +202,7 @@
         tap_rows[CH * b : CH * (b + 1), :] = tap_values[:, W * b : W * (b + 1)]
     tap_flip[...] = dot(tap_rows[...].astype(BF16), flip)
 
-    def convolve(c, carry):
+    for c in range(CH):
         both = scale * toeplitz_sum(
             n,
             lambda b: tap_flip[pl.ds(CH * b + c, 1), :],
@@ -193,11 +216,9 @@
         )
         wide2[pl.ds(c, n, stride=8), :] = both[n:]
         wide2[pl.ds(CH + c, n, stride=8), :] = both[:n]
-        return carry
-
-    lax.fori_loop(0, CH, convolve, 0)
     send2[...] = wide2[...].reshape(n, 8, W).astype(BF16)
-    exchange("seq", me_seq, send2, recv2, 2)
+    exchange_seq(send2, recv2, 2)
+    pl.when(jnp.logical_not(late))(exchange_lags)
 
     all_of("seq", me_seq, send2, recv2, 2).wait_recv()
     came = recv2[...].astype(F32).reshape(CH * n // 8, 2, 8, W)
@@ -209,8 +230,6 @@
     qgrad_ref[...] = (g[...].astype(F32) * conv).astype(BF16)
     kgrad_ref[...] = (back * v[...].astype(F32)).astype(BF16)
     vgrad_ref[...] = (back * k[...].astype(F32)).astype(BF16)
-
-    pl.when(jnp.logical_not(late))(exchange_lags)
 
     all_of("seq", me_seq, send1, recv1, 0).wait_send()
     all_of("seq", me_seq, send2, recv2, 2).wait_send()

time: 44.5 us -> 36 us (0.81)
  Pallas kernels: 43.7 us -> 35.2 us
    pallas_call x1, Pallas kernels: 43 us -> 34.5 us  [on_device(): pl.pallas_call(functools.partial(kernel, n, 1.0 / math.sqrt(length)), out...]
where the time goes in v2:
time: 36 us; the launch traced here: 35.9 us
  Pallas kernels  35.2 us (98%)
  between operations  0.64 us (2%)
    pallas_call x1, Pallas kernels, on_device(): pl.pallas_call(functools.partial(kernel, n, 1.0 / math.sqrt(length)), out...  34.5 us

profile of v2, /device:TPU:1, one launch (start us, length us, event | category | flops | bytes accessed | tf_op | source)
XLA Modules:
  0.0 35.9 jit_solution(10805181932483341173)
XLA Ops:
  0.6 34.5 %shard_map.92 = (bf16[128,128]{1,0:T(8,128)(2,1)S(1)}, bf16[128,128]{1,0:T(8,128)(2,1)S(1)}, bf16[128,128]{1,0:T(8,128)(2,1)S(1)}, bf16[128,128]{1,0:T(8,128)(2,1)S(1)}, f32[4,128]{1,0:T(4,128)S(1)}) custom-call(bf16[128,128]{1,0:T(8,128)(2,1)} %q_hbm.1, bf16[128,128]{1,0:T(8,128)(2,1)} %k_hbm.1, bf16[128,128]{1,0:T(8,128)(2,1)} %v_hbm.1, ...), custom_call_target="tpu_custom_call" | custom-call | tf_op jit(solution)/shard_map/pallas_call | solution.py:260
  35.2 0.7 %shard_map.93 = (bf16[128,128]{1,0:T(8,128)(2,1)}, bf16[128,128]{1,0:T(8,128)(2,1)}, bf16[128,128]{1,0:T(8,128)(2,1)}, bf16[128,128]{1,0:T(8,128)(2,1)}, f32[4,128]{1,0:T(4,128)}) custom-call(bf16[128,128]{1,0:T(8,128)(2,1)S(1)} %get-tuple-element.10.refs_0_, bf16[128,128]{1,0:T(8,128)(2,1)S(1)} %get-tuple-element.11.refs_1_, ...), custom_call_target="tpu_custom_call" | custom-call | tf_op jit(solution)/shard_map/pallas_call | solution.py:290

commit v3 on v2

--- a/solution.py
+++ b/solution.py
@@ -57,7 +57,38 @@
     me_chan = lax.axis_index("chan")
     core = lax.rem(me_seq, 2)
     pair = me_seq + 1 - 2 * core
-    late = me_chan >= n // 2
+    lags_turn = jnp.where(me_chan >= 3 * n // 8, 0, 1)
+    last = me_chan >= 3 * n // 4
+
+    barrier = pltpu.get_barrier_semaphore()
+
+    def tell(sem, **to):
+        pl.semaphore_signal(sem, inc=1, device_id=to, device_id_type=MESH)
+
+    chips = n // 2
+    outer = min(chips, 4)
+    inner = chips // outer
+    own = (inner // 2) * outer + outer // 2
+    my_outer, my_inner = me_seq // (2 * inner), lax.rem(me_seq // 2, inner)
+
+    def chip_at(i):
+        at_outer = lax.rem(my_outer + outer // 2 + lax.rem(i, outer), outer)
+        at_inner = lax.rem(my_inner + inner // 2 + i // outer, inner)
+        return 2 * (at_outer * inner + at_inner)
+
+    def each_other_chip(step):
+        def body(i, carry):
+            step(chip_at(i))
+            return carry
+
+        lax.fori_loop(0, own, body, 0)
+        lax.fori_loop(own + 1, chips, body, 0)
+
+    each_other_chip(lambda to: tell(barrier, seq=to))
+
+    @pl.when(core == 1)
+    def _():
+        tell(barrier, seq=pair)
 
     loads = [
         pltpu.make_async_copy(src, dst, in_sem.at[i])
@@ -67,36 +98,6 @@
     ]
     for load in loads:
         load.start()
-
-    barrier = pltpu.get_barrier_semaphore()
-
-    def tell(sem, **to):
-        pl.semaphore_signal(sem, inc=1, device_id=to, device_id_type=MESH)
-
-    chips = n // 2
-    outer = min(chips, 4)
-    inner = chips // outer
-    own = (inner // 2) * outer + outer // 2
-    my_outer, my_inner = me_seq // (2 * inner), lax.rem(me_seq // 2, inner)
-
-    def chip_at(i):
-        at_outer = lax.rem(my_outer + outer // 2 + lax.rem(i, outer), outer)
-        at_inner = lax.rem(my_inner + inner // 2 + i // outer, inner)
-        return 2 * (at_outer * inner + at_inner)
-
-    def each_other_chip(step):
-        def body(i, carry):
-            step(chip_at(i))
-            return carry
-
-        lax.fori_loop(0, own, body, 0)
-        lax.fori_loop(own + 1, chips, body, 0)
-
-    each_other_chip(lambda to: tell(barrier, seq=to))
-
-    @pl.when(core == 1)
-    def _():
-        tell(barrier, seq=pair)
 
     def greet_chan(i, carry):
         tell(barrier, seq=me_seq - core + 1, chan=i)
@@ -168,57 +169,66 @@
     pad_p[...] = jnp.zeros_like(pad_p)
     pad_x[...] = jnp.zeros_like(pad_x)
 
+    loads[4].wait()
+    tap_values = taps[...].astype(F32)
+    for b in range(n):
+        tap_rows[CH * b : CH * (b + 1), :] = tap_values[:, W * b : W * (b + 1)]
+    tap_flip[...] = dot(tap_rows[...].astype(BF16), flip)
+
     all_of("seq", me_seq, send1, recv1, 0).wait_recv()
     wide1[...] = recv1[...].reshape(n * 8, W).astype(F32)
     for c in range(CH):
         pad_p[c, :n, :] = wide1[pl.ds(CH + c, n, stride=8), :]
         pad_x[c, n:, :] = wide1[pl.ds(c, n, stride=8), :]
 
-    for c in range(CH):
-        wide3[pl.ds(c, n, stride=8), :] = scale * toeplitz_sum(
-            n,
-            lambda b: pad_x[c, pl.ds(n + b, 1), :],
-            lambda b: pad_p[c, b : b + n, :].astype(BF16),
-        )
-    send3[...] = wide3[...].reshape(n, 8, W)[:, :CH, :]
-
-    def exchange_lags():
+    def pass_chan_on():
         @pl.when(core == 1)
         def _():
             pl.semaphore_wait(barrier, 2 * (n - 1))
             tell(all_chan, seq=pair)
 
+    def lags():
+        for c in range(CH):
+            wide3[pl.ds(c, n, stride=8), :] = scale * toeplitz_sum(
+                n,
+                lambda b: pad_x[c, pl.ds(n + b, 1), :],
+                lambda b: pad_p[c, b : b + n, :].astype(BF16),
+            )
+        send3[...] = wide3[...].reshape(n, 8, W)[:, :CH, :]
+        pl.when(jnp.logical_not(last))(pass_chan_on)
+
         @pl.when(core == 0)
         def _():
             pl.semaphore_wait(all_chan, 1)
 
         exchange_chan(send3, recv3, 4)
 
-    pl.when(late)(exchange_lags)
-
-    loads[4].wait()
-    tap_values = taps[...].astype(F32)
-    for b in range(n):
-        tap_rows[CH * b : CH * (b + 1), :] = tap_values[:, W * b : W * (b + 1)]
-    tap_flip[...] = dot(tap_rows[...].astype(BF16), flip)
-
-    for c in range(CH):
-        both = scale * toeplitz_sum(
-            n,
-            lambda b: tap_flip[pl.ds(CH * b + c, 1), :],
-            lambda b: jnp.concatenate(
-                [
-                    pad_p[c, b : b + n, :].astype(BF16),
-                    pad_x[c, n - b : 2 * n - b, :].astype(BF16),
-                ],
-                axis=0,
-            ),
-        )
-        wide2[pl.ds(c, n, stride=8), :] = both[n:]
-        wide2[pl.ds(CH + c, n, stride=8), :] = both[:n]
-    send2[...] = wide2[...].reshape(n, 8, W).astype(BF16)
-    exchange_seq(send2, recv2, 2)
-    pl.when(jnp.logical_not(late))(exchange_lags)
+    def convolutions():
+        for c in range(CH):
+            both = scale * toeplitz_sum(
+                n,
+                lambda b: tap_flip[pl.ds(CH * b + c, 1), :],
+                lambda b: jnp.concatenate(
+                    [
+                        pad_p[c, b : b + n, :].astype(BF16),
+                        pad_x[c, n - b : 2 * n - b, :].astype(BF16),
+                    ],
+                    axis=0,
+                ),
+            )
+            wide2[pl.ds(c, n, stride=8), :] = both[n:]
+            wide2[pl.ds(CH + c, n, stride=8), :] = both[:n]
+        send2[...] = wide2[...].reshape(n, 8, W).astype(BF16)
+        exchange_seq(send2, recv2, 2)
+
+    pl.when(last)(pass_chan_on)
+
+    def turn(i, carry):
+        pl.when(i == lags_turn)(lags)
+        pl.when(i != lags_turn)(convolutions)
+        return carry
+
+    lax.fori_loop(0, 2, turn, 0)
 
     all_of("seq", me_seq, send2, recv2, 2).wait_recv()
     came = recv2[...].astype(F32).reshape(CH * n // 8, 2, 8, W)

time: 36 us -> 36.1 us (level)
  no operation moved by 1% of the time
where the time goes in v3:
time: 36.1 us; the launch traced here: 35.9 us
  Pallas kernels  35.3 us (98%)
  between operations  0.64 us (2%)
    pallas_call x1, Pallas kernels, on_device(): pl.pallas_call(functools.partial(kernel, n, 1.0 / math.sqrt(length)), out...  34.6 us

profile of v3, /device:TPU:1, one launch (start us, length us, event | category | flops | bytes accessed | tf_op | source)
XLA Modules:
  0.0 35.9 jit_solution(14488989828990488144)
XLA Ops:
  0.6 34.6 %shard_map.92 = (bf16[128,128]{1,0:T(8,128)(2,1)S(1)}, bf16[128,128]{1,0:T(8,128)(2,1)S(1)}, bf16[128,128]{1,0:T(8,128)(2,1)S(1)}, bf16[128,128]{1,0:T(8,128)(2,1)S(1)}, f32[4,128]{1,0:T(4,128)S(1)}) custom-call(bf16[128,128]{1,0:T(8,128)(2,1)} %q_hbm.1, bf16[128,128]{1,0:T(8,128)(2,1)} %k_hbm.1, bf16[128,128]{1,0:T(8,128)(2,1)} %v_hbm.1, ...), custom_call_target="tpu_custom_call" | custom-call | tf_op jit(solution)/shard_map/pallas_call | solution.py:270
  35.2 0.7 %shard_map.93 = (bf16[128,128]{1,0:T(8,128)(2,1)}, bf16[128,128]{1,0:T(8,128)(2,1)}, bf16[128,128]{1,0:T(8,128)(2,1)}, bf16[128,128]{1,0:T(8,128)(2,1)}, f32[4,128]{1,0:T(4,128)}) custom-call(bf16[128,128]{1,0:T(8,128)(2,1)S(1)} %get-tuple-element.10.refs_0_, bf16[128,128]{1,0:T(8,128)(2,1)S(1)} %get-tuple-element.11.refs_1_, ...), custom_call_target="tpu_custom_call" | custom-call | tf_op jit(solution)/shard_map/pallas_call | solution.py:300

commit v4 on v3

--- a/solution.py
+++ b/solution.py
@@ -12,6 +12,7 @@
 F32 = jnp.float32
 BF16 = jnp.bfloat16
 W = 128
+G = 32
 CH = 4
 
 
@@ -45,20 +46,64 @@
     return total
 
 
+def shifted_rows(rows_of, turned):
+    lane = lax.broadcasted_iota(jnp.int32, (rows_of, W), 1)
+    return [
+        jnp.where(
+            lane < 2 * G,
+            jnp.where(lane < G, turned(-r % 4, 0), turned((1 - r) % 4, 1)),
+            jnp.where(lane < 3 * G, turned((2 - r) % 4, 2), turned((3 - r) % 4, 3)),
+        )
+        for r in range(4)
+    ]
+
+
+def lag_sum(blocks, row_of, left_of):
+    row = lax.broadcasted_iota(jnp.int32, (G, W), 0)
+    col = lax.broadcasted_iota(jnp.int32, (G, W), 1)
+    lower = row >= col
+    before = jnp.zeros((G, W), F32)
+    bases = []
+    for k in range(blocks + 1):
+        if k < blocks:
+            turned = pltpu.roll(
+                jnp.broadcast_to(row_of(k), (G, W)), 1, 1, stride=1, stride_axis=0
+            )
+        else:
+            turned = jnp.zeros((G, W), F32)
+        bases.append(jnp.where(lower, turned, before).astype(BF16))
+        before = turned
+    total = None
+    step = min(blocks, 8)
+    for k in range(0, blocks, step):
+        right = jnp.concatenate(
+            [jnp.concatenate([bases[b + 1], bases[b]], axis=1) for b in range(k, k + step)], axis=0
+        )
+        left = jnp.concatenate([left_of(t) for t in range(k // 4, (k + step) // 4)], axis=1)
+        term = dot(left, right)
+        total = term if total is None else total + term
+    lane = lax.broadcasted_iota(jnp.int32, (blocks, W), 1)
+    out = total[:blocks, W:]
+    for r in range(1, 4):
+        part = total[r * blocks : (r + 1) * blocks]
+        chosen = jnp.where(lane < W - G * r, part[:, W:], part[:, :W])
+        out = out + pltpu.roll(chosen, G * r, 1)
+    return out
+
+
 def kernel(
     n, scale,
     q_hbm, k_hbm, v_hbm, g_hbm, taps_hbm,
     gated_ref, qgrad_ref, kgrad_ref, vgrad_ref, fgrad_ref,
     q, k, v, g, taps, in_sem,
     send1, recv1, send2, recv2, send3, recv3, sems, all_seq, all_chan,
-    tap_rows, tap_flip, wide1, pad_p, pad_x, wide2, wide3,
+    tap_rows, tap_flip, wide1, pad_p, pad_x, wide2, wide3, turned_p, pad_q,
 ):
     me_seq = lax.axis_index("seq")
     me_chan = lax.axis_index("chan")
     core = lax.rem(me_seq, 2)
     pair = me_seq + 1 - 2 * core
     lags_turn = jnp.where(me_chan >= 3 * n // 8, 0, 1)
-    last = me_chan >= 3 * n // 4
 
     barrier = pltpu.get_barrier_semaphore()
 
@@ -100,11 +145,13 @@
         load.start()
 
     def greet_chan(i, carry):
-        tell(barrier, seq=me_seq - core + 1, chan=i)
+        @pl.when(i != me_chan)
+        def _():
+            tell(barrier, seq=me_seq - core + 1, chan=i)
+
         return carry
 
-    lax.fori_loop(0, me_chan, greet_chan, 0)
-    lax.fori_loop(me_chan + 1, n, greet_chan, 0)
+    lax.fori_loop(n // 4, 3 * n // 4, greet_chan, 0)
 
     half = lax.broadcasted_iota(jnp.int32, (CH * n // 8, 8, W), 1) < CH
     flip = flip_matrix()
@@ -165,9 +212,13 @@
         )
 
     exchange_seq(send1, recv1, 0)
+    lax.fori_loop(0, n // 4, greet_chan, 0)
+    lax.fori_loop(3 * n // 4, n, greet_chan, 0)
 
     pad_p[...] = jnp.zeros_like(pad_p)
     pad_x[...] = jnp.zeros_like(pad_x)
+    pad_q[...] = jnp.zeros_like(pad_q)
+    turned_p[...] = jnp.zeros_like(turned_p)
 
     loads[4].wait()
     tap_values = taps[...].astype(F32)
@@ -188,15 +239,24 @@
             tell(all_chan, seq=pair)
 
     def lags():
+        pass_chan_on()
         for c in range(CH):
-            wide3[pl.ds(c, n, stride=8), :] = scale * toeplitz_sum(
+            for s in range(4):
+                own_rows = pad_p[c, :n, :]
+                turned_p[s, c, :n, :] = pltpu.roll(own_rows, G * s, 1) if s else own_rows
+        for c in range(CH):
+            for r, rows in enumerate(
+                shifted_rows(n, lambda s, j: turned_p[s, c, j : j + n, :])
+            ):
+                pad_q[c, r, :n, :] = rows
+            wide3[pl.ds(c, n, stride=8), :] = scale * lag_sum(
                 n,
                 lambda b: pad_x[c, pl.ds(n + b, 1), :],
-                lambda b: pad_p[c, b : b + n, :].astype(BF16),
+                lambda t: jnp.concatenate(
+                    [pad_q[c, r, 4 * t : 4 * t + n, :].astype(BF16) for r in range(4)], axis=0
+                ),
             )
         send3[...] = wide3[...].reshape(n, 8, W)[:, :CH, :]
-        pl.when(jnp.logical_not(last))(pass_chan_on)
-
         @pl.when(core == 0)
         def _():
             pl.semaphore_wait(all_chan, 1)
@@ -220,8 +280,6 @@
             wide2[pl.ds(CH + c, n, stride=8), :] = both[:n]
         send2[...] = wide2[...].reshape(n, 8, W).astype(BF16)
         exchange_seq(send2, recv2, 2)
-
-    pl.when(last)(pass_chan_on)
 
     def turn(i, carry):
         pl.when(i == lags_turn)(lags)
@@ -292,6 +350,8 @@
             pltpu.VMEM((CH, 2 * n, W), F32),
             pltpu.VMEM((8 * n, W), F32),
             pltpu.VMEM((8 * n, W), F32),
+            pltpu.VMEM((4, CH, n + 8, W), F32),
+            pltpu.VMEM((CH, 4, 2 * n, W), F32),
         ],
         compiler_params=pltpu.CompilerParams(
             collective_id=0, has_side_effects=True, vmem_limit_bytes=32 << 20

time: 36.1 us -> 35.7 us (0.989)
  Pallas kernels: 35.3 us -> 34.8 us
    pallas_call x1, Pallas kernels: 34.6 us -> 34.1 us  [on_device(): pl.pallas_call(functools.partial(kernel, n, 1.0 / math.sqrt(length)), out...]
where the time goes in v4:
time: 35.7 us; the launch traced here: 35.4 us
  Pallas kernels  34.8 us (97%)
  between operations  0.64 us (2%)
    pallas_call x1, Pallas kernels, on_device(): pl.pallas_call(functools.partial(kernel, n, 1.0 / math.sqrt(length)), out...  34.1 us

profile of v4, /device:TPU:1, one launch (start us, length us, event | category | flops | bytes accessed | tf_op | source)
XLA Modules:
  0.0 35.4 jit_solution(5902358835710007373)
XLA Ops:
  0.6 34.1 %shard_map.92 = (bf16[128,128]{1,0:T(8,128)(2,1)S(1)}, bf16[128,128]{1,0:T(8,128)(2,1)S(1)}, bf16[128,128]{1,0:T(8,128)(2,1)S(1)}, bf16[128,128]{1,0:T(8,128)(2,1)S(1)}, f32[4,128]{1,0:T(4,128)S(1)}) custom-call(bf16[128,128]{1,0:T(8,128)(2,1)} %q_hbm.1, bf16[128,128]{1,0:T(8,128)(2,1)} %k_hbm.1, bf16[128,128]{1,0:T(8,128)(2,1)} %v_hbm.1, ...), custom_call_target="tpu_custom_call" | custom-call | tf_op jit(solution)/shard_map/pallas_call | solution.py:328
  34.7 0.7 %shard_map.93 = (bf16[128,128]{1,0:T(8,128)(2,1)}, bf16[128,128]{1,0:T(8,128)(2,1)}, bf16[128,128]{1,0:T(8,128)(2,1)}, bf16[128,128]{1,0:T(8,128)(2,1)}, f32[4,128]{1,0:T(4,128)}) custom-call(bf16[128,128]{1,0:T(8,128)(2,1)S(1)} %get-tuple-element.10.refs_0_, bf16[128,128]{1,0:T(8,128)(2,1)S(1)} %get-tuple-element.11.refs_1_, ...), custom_call_target="tpu_custom_call" | custom-call | tf_op jit(solution)/shard_map/pallas_call | solution.py:360

commit v5 on v4

--- a/solution.py
+++ b/solution.py
@@ -101,39 +101,9 @@
 ):
     me_seq = lax.axis_index("seq")
     me_chan = lax.axis_index("chan")
-    core = lax.rem(me_seq, 2)
-    pair = me_seq + 1 - 2 * core
+    core = 1 - lax.rem(me_seq, 2)
+    pair = me_seq - 1 + 2 * core
     lags_turn = jnp.where(me_chan >= 3 * n // 8, 0, 1)
-
-    barrier = pltpu.get_barrier_semaphore()
-
-    def tell(sem, **to):
-        pl.semaphore_signal(sem, inc=1, device_id=to, device_id_type=MESH)
-
-    chips = n // 2
-    outer = min(chips, 4)
-    inner = chips // outer
-    own = (inner // 2) * outer + outer // 2
-    my_outer, my_inner = me_seq // (2 * inner), lax.rem(me_seq // 2, inner)
-
-    def chip_at(i):
-        at_outer = lax.rem(my_outer + outer // 2 + lax.rem(i, outer), outer)
-        at_inner = lax.rem(my_inner + inner // 2 + i // outer, inner)
-        return 2 * (at_outer * inner + at_inner)
-
-    def each_other_chip(step):
-        def body(i, carry):
-            step(chip_at(i))
-            return carry
-
-        lax.fori_loop(0, own, body, 0)
-        lax.fori_loop(own + 1, chips, body, 0)
-
-    each_other_chip(lambda to: tell(barrier, seq=to))
-
-    @pl.when(core == 1)
-    def _():
-        tell(barrier, seq=pair)
 
     loads = [
         pltpu.make_async_copy(src, dst, in_sem.at[i])
@@ -141,17 +111,50 @@
             ((k_hbm, k), (v_hbm, v), (g_hbm, g), (q_hbm, q), (taps_hbm, taps))
         )
     ]
-    for load in loads:
+    for load in loads[:4]:
         load.start()
+
+    barrier = pltpu.get_barrier_semaphore()
+
+    def tell(sem, **to):
+        pl.semaphore_signal(sem, inc=1, device_id=to, device_id_type=MESH)
+
+    chips = n // 2
+    outer = min(chips, 4)
+    inner = chips // outer
+    own = (inner // 2) * outer + outer // 2
+    my_outer, my_inner = me_seq // (2 * inner), lax.rem(me_seq // 2, inner)
+
+    def chip_at(i):
+        at_outer = lax.rem(my_outer + outer // 2 + lax.rem(i, outer), outer)
+        at_inner = lax.rem(my_inner + inner // 2 + i // outer, inner)
+        return 2 * (at_outer * inner + at_inner)
+
+    def each_other_chip(step):
+        def body(i, carry):
+            step(chip_at(i))
+            return carry
+
+        lax.fori_loop(0, own, body, 0)
+        lax.fori_loop(own + 1, chips, body, 0)
+
+    each_other_chip(lambda to: tell(barrier, seq=to + 1))
+
+    @pl.when(core == 1)
+    def _():
+        tell(barrier, seq=pair)
+
+    loads[4].start()
 
     def greet_chan(i, carry):
         @pl.when(i != me_chan)
         def _():
-            tell(barrier, seq=me_seq - core + 1, chan=i)
+            tell(barrier, seq=me_seq - 1 + core, chan=i)
 
         return carry
 
-    lax.fori_loop(n // 4, 3 * n // 4, greet_chan, 0)
+    lax.fori_loop(n // 2, 3 * n // 4, greet_chan, 0)
+    lax.fori_loop(n // 4, n // 2, greet_chan, 0)
 
     half = lax.broadcasted_iota(jnp.int32, (CH * n // 8, 8, W), 1) < CH
     flip = flip_matrix()
@@ -239,7 +242,7 @@
             tell(all_chan, seq=pair)
 
     def lags():
-        pass_chan_on()
+        pl.when(me_chan >= n // 2)(pass_chan_on)
         for c in range(CH):
             for s in range(4):
                 own_rows = pad_p[c, :n, :]
@@ -256,6 +259,7 @@
                     [pad_q[c, r, 4 * t : 4 * t + n, :].astype(BF16) for r in range(4)], axis=0
                 ),
             )
+        pl.when(me_chan < n // 2)(pass_chan_on)
         send3[...] = wide3[...].reshape(n, 8, W)[:, :CH, :]
         @pl.when(core == 0)
         def _():

time: 35.7 us -> 35.7 us (level)
  no operation moved by 1% of the time
where the time goes in v5:
time: 35.7 us; the launch traced here: 35.4 us
  Pallas kernels  34.8 us (97%)
  between operations  0.64 us (2%)
    pallas_call x1, Pallas kernels, on_device(): pl.pallas_call(functools.partial(kernel, n, 1.0 / math.sqrt(length)), out...  34.1 us

profile of v5, /device:TPU:1, one launch (start us, length us, event | category | flops | bytes accessed | tf_op | source)
XLA Modules:
  0.0 35.4 jit_solution(16731439009086020449)
XLA Ops:
  0.6 34.1 %shard_map.92 = (bf16[128,128]{1,0:T(8,128)(2,1)S(1)}, bf16[128,128]{1,0:T(8,128)(2,1)S(1)}, bf16[128,128]{1,0:T(8,128)(2,1)S(1)}, bf16[128,128]{1,0:T(8,128)(2,1)S(1)}, f32[4,128]{1,0:T(4,128)S(1)}) custom-call(bf16[128,128]{1,0:T(8,128)(2,1)} %q_hbm.1, bf16[128,128]{1,0:T(8,128)(2,1)} %k_hbm.1, bf16[128,128]{1,0:T(8,128)(2,1)} %v_hbm.1, ...), custom_call_target="tpu_custom_call" | custom-call | tf_op jit(solution)/shard_map/pallas_call | solution.py:332
  34.7 0.7 %shard_map.93 = (bf16[128,128]{1,0:T(8,128)(2,1)}, bf16[128,128]{1,0:T(8,128)(2,1)}, bf16[128,128]{1,0:T(8,128)(2,1)}, bf16[128,128]{1,0:T(8,128)(2,1)}, f32[4,128]{1,0:T(4,128)}) custom-call(bf16[128,128]{1,0:T(8,128)(2,1)S(1)} %get-tuple-element.10.refs_0_, bf16[128,128]{1,0:T(8,128)(2,1)S(1)} %get-tuple-element.11.refs_1_, ...), custom_call_target="tpu_custom_call" | custom-call | tf_op jit(solution)/shard_map/pallas_call | solution.py:364

commit v6 on v5

--- a/solution.py
+++ b/solution.py
@@ -138,11 +138,11 @@
         lax.fori_loop(0, own, body, 0)
         lax.fori_loop(own + 1, chips, body, 0)
 
-    each_other_chip(lambda to: tell(barrier, seq=to + 1))
-
     @pl.when(core == 1)
     def _():
         tell(barrier, seq=pair)
+
+    each_other_chip(lambda to: tell(barrier, seq=to + 1))
 
     loads[4].start()
 
@@ -152,6 +152,12 @@
             tell(barrier, seq=me_seq - 1 + core, chan=i)
 
         return carry
+
+    far_side = my_inner == inner // 2
+
+    def greet_others():
+        lax.fori_loop(0, n // 4, greet_chan, 0)
+        lax.fori_loop(3 * n // 4, n, greet_chan, 0)
 
     lax.fori_loop(n // 2, 3 * n // 4, greet_chan, 0)
     lax.fori_loop(n // 4, n // 2, greet_chan, 0)
@@ -173,6 +179,8 @@
     )
     send1[...] = paired.reshape(n, 8, W).astype(BF16)
 
+    pl.when(jnp.logical_not(far_side))(greet_others)
+
     @pl.when(core == 0)
     def _():
         pl.semaphore_wait(barrier, n - 1)
@@ -215,8 +223,7 @@
         )
 
     exchange_seq(send1, recv1, 0)
-    lax.fori_loop(0, n // 4, greet_chan, 0)
-    lax.fori_loop(3 * n // 4, n, greet_chan, 0)
+    pl.when(far_side)(greet_others)
 
     pad_p[...] = jnp.zeros_like(pad_p)
     pad_x[...] = jnp.zeros_like(pad_x)

time: 35.7 us -> 35.7 us (level)
  no operation moved by 1% of the time
where the time goes in v6:
time: 35.7 us; the launch traced here: 35.4 us
  Pallas kernels  34.8 us (97%)
  between operations  0.64 us (2%)
    pallas_call x1, Pallas kernels, on_device(): pl.pallas_call(functools.partial(kernel, n, 1.0 / math.sqrt(length)), out...  34.1 us

profile of v6, /device:TPU:1, one launch (start us, length us, event | category | flops | bytes accessed | tf_op | source)
XLA Modules:
  0.0 35.4 jit_solution(5536748285897247815)
XLA Ops:
  0.6 34.1 %shard_map.92 = (bf16[128,128]{1,0:T(8,128)(2,1)S(1)}, bf16[128,128]{1,0:T(8,128)(2,1)S(1)}, bf16[128,128]{1,0:T(8,128)(2,1)S(1)}, bf16[128,128]{1,0:T(8,128)(2,1)S(1)}, f32[4,128]{1,0:T(4,128)S(1)}) custom-call(bf16[128,128]{1,0:T(8,128)(2,1)} %q_hbm.1, bf16[128,128]{1,0:T(8,128)(2,1)} %k_hbm.1, bf16[128,128]{1,0:T(8,128)(2,1)} %v_hbm.1, ...), custom_call_target="tpu_custom_call" | custom-call | tf_op jit(solution)/shard_map/pallas_call | solution.py:339
  34.7 0.7 %shard_map.93 = (bf16[128,128]{1,0:T(8,128)(2,1)}, bf16[128,128]{1,0:T(8,128)(2,1)}, bf16[128,128]{1,0:T(8,128)(2,1)}, bf16[128,128]{1,0:T(8,128)(2,1)}, f32[4,128]{1,0:T(4,128)}) custom-call(bf16[128,128]{1,0:T(8,128)(2,1)S(1)} %get-tuple-element.10.refs_0_, bf16[128,128]{1,0:T(8,128)(2,1)S(1)} %get-tuple-element.11.refs_1_, ...), custom_call_target="tpu_custom_call" | custom-call | tf_op jit(solution)/shard_map/pallas_call | solution.py:371

commit v7 on v6

--- a/solution.py
+++ b/solution.py
@@ -135,8 +135,8 @@
             step(chip_at(i))
             return carry
 
-        lax.fori_loop(0, own, body, 0)
-        lax.fori_loop(own + 1, chips, body, 0)
+        lax.fori_loop(0, own, body, 0, unroll=True)
+        lax.fori_loop(own + 1, chips, body, 0, unroll=True)
 
     @pl.when(core == 1)
     def _():
@@ -156,11 +156,11 @@
     far_side = my_inner == inner // 2
 
     def greet_others():
-        lax.fori_loop(0, n // 4, greet_chan, 0)
-        lax.fori_loop(3 * n // 4, n, greet_chan, 0)
-
-    lax.fori_loop(n // 2, 3 * n // 4, greet_chan, 0)
-    lax.fori_loop(n // 4, n // 2, greet_chan, 0)
+        lax.fori_loop(0, n // 4, greet_chan, 0, unroll=True)
+        lax.fori_loop(3 * n // 4, n, greet_chan, 0, unroll=True)
+
+    lax.fori_loop(n // 2, 3 * n // 4, greet_chan, 0, unroll=True)
+    lax.fori_loop(n // 4, n // 2, greet_chan, 0, unroll=True)
 
     half = lax.broadcasted_iota(jnp.int32, (CH * n // 8, 8, W), 1) < CH
     flip = flip_matrix()

time: 35.7 us -> 35.2 us (0.986)
  Pallas kernels: 34.8 us -> 34.4 us
    pallas_call x1, Pallas kernels: 34.1 us -> 33.7 us  [on_device(): pl.pallas_call(functools.partial(kernel, n, 1.0 / math.sqrt(length)), out...]
where the time goes in v7:
time: 35.2 us; the launch traced here: 35 us
  Pallas kernels  34.4 us (98%)
  between operations  0.64 us (2%)
    pallas_call x1, Pallas kernels, on_device(): pl.pallas_call(functools.partial(kernel, n, 1.0 / math.sqrt(length)), out...  33.7 us

profile of v7, /device:TPU:1, one launch (start us, length us, event | category | flops | bytes accessed | tf_op | source)
XLA Modules:
  0.0 35.0 jit_solution(1656129371237590534)
XLA Ops:
  0.6 33.7 %shard_map.92 = (bf16[128,128]{1,0:T(8,128)(2,1)S(1)}, bf16[128,128]{1,0:T(8,128)(2,1)S(1)}, bf16[128,128]{1,0:T(8,128)(2,1)S(1)}, bf16[128,128]{1,0:T(8,128)(2,1)S(1)}, f32[4,128]{1,0:T(4,128)S(1)}) custom-call(bf16[128,128]{1,0:T(8,128)(2,1)} %q_hbm.1, bf16[128,128]{1,0:T(8,128)(2,1)} %k_hbm.1, bf16[128,128]{1,0:T(8,128)(2,1)} %v_hbm.1, ...), custom_call_target="tpu_custom_call" | custom-call | tf_op jit(solution)/shard_map/pallas_call | solution.py:339
  34.3 0.7 %shard_map.93 = (bf16[128,128]{1,0:T(8,128)(2,1)}, bf16[128,128]{1,0:T(8,128)(2,1)}, bf16[128,128]{1,0:T(8,128)(2,1)}, bf16[128,128]{1,0:T(8,128)(2,1)}, f32[4,128]{1,0:T(4,128)}) custom-call(bf16[128,128]{1,0:T(8,128)(2,1)S(1)} %get-tuple-element.10.refs_0_, bf16[128,128]{1,0:T(8,128)(2,1)S(1)} %get-tuple-element.11.refs_1_, ...), custom_call_target="tpu_custom_call" | custom-call | tf_op jit(solution)/shard_map/pallas_call | solution.py:371
